TPU v7x, 256 devices: a whole 4x4x8 slice. The times are simulated.
256 devices in a mesh: track: 16 (over z, x_lo), tm: 16 (over x_hi, y, core).
Axes of the slice: x: 4 (x_hi: 2, x_lo: 2; x = x_hi * 2 + x_lo), y: 4, z: 8, core: 2. Of those that a mesh axis runs over, the one named last changes fastest.
Arguments:
- positions: float32 [3, 32, 6144], P(None, 'tm', 'track'), may hold values from -6 to 6
- embeddings: float32 [32, 128, 6144], P('tm', None, 'track'), may hold values from -6 to 6
- visible: int32 [32, 6144], P('tm', 'track'), may hold values 0 or 1
Outputs:
- grad_positions: float32 [3, 32, 6144], P(None, 'tm', 'track')
- grad_embeddings: float32 [32, 128, 6144], P('tm', None, 'track')
- mean_loss: float32 [], replicated
All inputs are finite; a program needn't handle non-finite values. No bound on the sum of `visible` on one device may be relied on, other than what follows from the above.
Results may differ from a plain program's by a relative error of at most 0.00014.
Values sent between devices are 32-bit elements; how exact they have to be, the bound alone decides.
A program may use at most 128 MiB of HBM per device.

v0:
```python
import math
import jax
import jax.numpy as jnp
from jax import lax
from jax.sharding import PartitionSpec as P

rigidity = 4.0
highest = lax.Precision.HIGHEST


def shifted(array, axis, by):
    size = lax.axis_size(axis)
    pairs = [(i, i + by) for i in range(size) if 0 <= i + by < size]
    return lax.ppermute(array, axis, pairs)


def tile_terms(pos_a, mask_a, emb_a, pos_b, mask_b, emb_b, weight_scale):
    inv_root = 1.0 / math.sqrt(emb_a.shape[1])
    offset = pos_a[:, :, :, None] - pos_b[:, :, None, :]
    distance = jnp.sqrt(jnp.sum(offset * offset, axis=0) + 1.0)
    change = distance[1:] - distance[:-1]
    both_seen = mask_a[:, :, None] * mask_b[:, None, :]
    seen_pair = both_seen[1:] * both_seen[:-1]
    logits = jnp.einsum("fei,fej->fij", emb_a, emb_b, precision=highest) * inv_root
    affinity = jax.nn.sigmoid(logits)
    squared = seen_pair * change * change
    energy = jnp.sum(affinity * squared)
    grad_change = 2.0 * weight_scale * affinity * seen_pair * change
    padding = jnp.zeros_like(grad_change[:1])
    grad_dist = jnp.concatenate([padding, grad_change], 0) - jnp.concatenate(
        [grad_change, padding], 0
    )
    scaled = (grad_dist / distance)[None] * offset
    grad_pos_a = jnp.sum(scaled, axis=3)
    grad_pos_b = -jnp.sum(scaled, axis=2)
    grad_logit = weight_scale * squared * affinity * (1.0 - affinity) * inv_root
    grad_emb_a = jnp.einsum("fij,fej->fei", grad_logit, emb_b, precision=highest)
    grad_emb_b = jnp.einsum("fij,fei->fej", grad_logit, emb_a, precision=highest)
    return (energy, grad_pos_a, grad_emb_a, grad_pos_b, grad_emb_b)


def on_device(positions, embeddings, visible):
    frames_local = embeddings.shape[0]
    block_width = embeddings.shape[2]
    tracks = block_width * lax.axis_size("track")
    frames = frames_local * lax.axis_size("tm")
    weight_scale = rigidity / math.sqrt(tracks)
    seen_mask = visible.astype(jnp.float32)
    next_pos, next_mask = shifted((positions[:, :1], seen_mask[:1]), "tm", -1)
    pos_ext = jnp.concatenate([positions, next_pos], 1)
    mask_ext = jnp.concatenate([seen_mask, next_mask], 0)
    packed = jnp.concatenate([pos_ext, mask_ext[None]], 0)

    def own_tile(others_packed, others_emb):
        return tile_terms(
            pos_ext,
            mask_ext,
            embeddings,
            others_packed[:3],
            others_packed[3],
            others_emb,
            weight_scale,
        )

    initial = (jnp.zeros_like(pos_ext), jnp.zeros_like(embeddings), jnp.zeros((), jnp.float32))
    piece_packed = lax.all_gather(packed, "track", axis=2, tiled=True)
    piece_emb = lax.all_gather(embeddings, "track", axis=2, tiled=True)
    columns = piece_emb.shape[2]
    blocks = columns // block_width
    split_packed = jnp.moveaxis(
        piece_packed.reshape(4, frames_local + 1, blocks, block_width), 2, 0
    )
    split_emb = jnp.moveaxis(
        piece_emb.reshape(frames_local, piece_emb.shape[1], blocks, block_width), 2, 0
    )

    def advance(inner, others):
        energy, grad_pos_a, grad_emb_a, unused_pos, unused_emb = own_tile(others[0], others[1])
        return ((inner[0] + grad_pos_a, inner[1] + grad_emb_a, inner[2] + energy), None)

    result, unused = lax.scan(advance, initial, (split_packed, split_emb))
    grad_pos, grad_emb, energy_sum = result
    energy_sum = 0.5 * energy_sum
    incoming = shifted(grad_pos[:, -1:], "tm", 1)
    grad_positions = grad_pos[:, :-1]
    grad_positions = jnp.concatenate([grad_positions[:, :1] + incoming, grad_positions[:, 1:]], 1)
    total = lax.psum(energy_sum, ("track", "tm"))
    mean_loss = total / (tracks * (tracks - 1) / 2.0 * (frames - 1))
    return (grad_positions, grad_emb, mean_loss)


def solution(mesh):
    in_specs = (P(None, "tm", "track"), P("tm", None, "track"), P("tm", "track"))
    out_specs = (P(None, "tm", "track"), P("tm", None, "track"), P())
    return jax.shard_map(
        on_device, mesh=mesh, in_specs=in_specs, out_specs=out_specs, check_vma=False
    )
```

profile of v0, /device:TPU:1, one launch (start us, length us, event | category | flops | bytes accessed | tf_op | source)
XLA Modules:
  0.0 581.3 jit_solution(791380038999158030)
XLA Ops:
  7.2 1.9 copy.30
  9.9 5.1 collective-permute-start
  15.7 1.9 collective-permute-start.1
  17.6 3.0 collective-permute-done.1
  21.3 41.1 %all_gather.7 = f32[4,3,6144]{2,1,0:T(4,128)S(1)} all-gather(f32[4,3,384]{2,1,0:T(4,128)S(1)} %pad_maximum_fusion), channel_id=1, replica_groups=mesh['track'=16,'tm'=16] {'track'}, dimensions={2}, use_global_device_ids=true | all-gather | bytes 313344 | tf_op jit(solution)/shard_map/all_gather | solution.py:66
  63.9 97.0 %all-gather.2.cloned.1.call-done = f32[2,128,6144]{1,2,0:T(8,128)} async-done(((f32[2,128,384]{1,2,0:T(8,128)}), f32[2,128,6144]{1,2,0:T(8,128)}) %all-gather.2.cloned.1.call-update) | async-done | bytes 6291472 | tf_op jit(solution)/shard_map/all_gather | solution.py:67
  160.9 327.7 %while.15 = (s32[]{:T(128)}, f32[3,3,384]{2,1,0:T(4,128)}, f32[2,128,384]{2,1,0:T(8,128)}, f32[]{:T(128)}, f32[16,2,128,384]{2,3,0,1:T(8,128)}, /*index=5*/f32[2...) while((s32[]{:T(128)}, f32[3,3,384]{2,1,0:T(4,128)}, ...), condition=%wide.region_4.5_spmd.clone, body=%wide.region_0.4_spmd.clone.sunk | while | flops 922389888 | bytes 49315164 | solution.py:81
  167.0 5.0 multiply_reduce_fusion.2
  172.7 4.3 convolution_add_fusion.2
  178.9 1.8 fusion.35
  183.7 1.6 fusion.34
  187.4 5.0 multiply_reduce_fusion.2
  193.2 4.4 convolution_add_fusion.2
  199.4 1.8 fusion.35
  204.1 1.6 fusion.34
  207.9 5.0 multiply_reduce_fusion.2
  213.6 4.4 convolution_add_fusion.2
  219.9 1.8 fusion.35
  224.6 1.6 fusion.34
  228.4 5.0 multiply_reduce_fusion.2
  234.1 4.4 convolution_add_fusion.2
  240.4 1.8 fusion.35
  248.9 5.0 multiply_reduce_fusion.2
  254.6 4.4 convolution_add_fusion.2
  260.9 1.8 fusion.35
  265.6 1.6 fusion.34
  269.4 5.0 multiply_reduce_fusion.2
  275.1 4.4 convolution_add_fusion.2
  281.3 1.8 fusion.35
  286.1 1.6 fusion.34
  289.9 5.0 multiply_reduce_fusion.2
  295.6 4.4 convolution_add_fusion.2
  301.8 1.8 fusion.35
  306.6 1.6 fusion.34
  310.3 5.0 multiply_reduce_fusion.2
  316.1 4.4 convolution_add_fusion.2
  322.3 1.8 fusion.35
  330.8 5.0 multiply_reduce_fusion.2
  336.6 4.4 convolution_add_fusion.2
  342.8 1.8 fusion.35
  347.6 1.6 fusion.34
  351.3 5.0 multiply_reduce_fusion.2
  357.1 4.4 convolution_add_fusion.2
  363.3 1.8 fusion.35
  371.8 5.0 multiply_reduce_fusion.2
  377.5 4.4 convolution_add_fusion.2
  383.8 1.8 fusion.35
  392.3 5.0 multiply_reduce_fusion.2
  398.0 4.4 convolution_add_fusion.2
  404.3 1.8 fusion.35
  412.8 5.0 multiply_reduce_fusion.2
  418.5 4.4 convolution_add_fusion.2
  424.8 1.8 fusion.35
  433.3 5.0 multiply_reduce_fusion.2
  439.0 4.4 convolution_add_fusion.2
  445.2 1.8 fusion.35
  453.7 5.0 multiply_reduce_fusion.2
  459.5 4.4 convolution_add_fusion.2
  465.7 1.8 fusion.35
  474.2 5.0 multiply_reduce_fusion.2
  480.0 4.4 convolution_add_fusion.2
  486.2 1.8 fusion.35
  489.4 4.8 collective-permute-start.2
  494.2 77.0 %psum.7 = f32[]{:T(128)} all-reduce(f32[]{:T(128)S(6)} %mul_shard_map.3), channel_id=1, replica_groups=mesh['track'=16,'tm'=16] {'track','tm'}, use_global_device_ids=true, to_apply=%region_5.6 | all-reduce | flops 1 | bytes 8 | tf_op jit(solution)/shard_map/psum | solution.py:87
  (363 shorter events, 130.1 us)
Async XLA Ops:
  7.2 56.1 %copy-start.6 = (f32[3,2,384]{2,1,0:T(2,128)S(1)}, f32[3,2,384]{2,1,0:T(2,128)}, u32[]{:S(2)}) copy-start(f32[3,2,384]{2,1,0:T(2,128)} %param.5) | copy-start | bytes 27652
  7.2 153.8 %all-gather.2.cloned.1.call-start = ((), (), s32[]{:S(2)}) async-start(), calls=%async_computation | async-start | bytes 6684672 | tf_op jit(solution)/shard_map/all_gather | solution.py:67
  9.9 7.7 %collective-permute-start = (f32[1,384]{1,0:T(1,128)S(1)}, f32[1,384]{1,0:T(1,128)S(1)}, u32[]{:S(2)}, u32[]{:S(2)}) collective-permute-start(f32[1,384]{1,0:T(1,128)S(1)} %slice.53), channel_id=1, source_target_pairs={{1,0},{2,1},{3,2},{4,3},{5,4},{6,5},{7,6},{8,7},{9,8},{10,9},{11,1... | collective-permute-start | bytes 4616 | tf_op jit(solution)/shard_map/ppermute | solution.py:14
  15.7 4.9 collective-permute-start.1
  166.0 1.0 copy-start.5
  166.7 5.4 copy-start
  172.7 4.3 copy-start.1
  178.9 1.8 copy-start.3
  186.4 1.0 copy-start.5
  187.1 5.4 copy-start
  193.1 4.4 copy-start.1
  199.4 1.8 copy-start.3
  206.9 1.0 copy-start.5
  207.6 5.4 copy-start
  213.6 4.4 copy-start.1
  219.9 1.8 copy-start.3
  227.4 1.0 copy-start.5
  228.0 5.4 copy-start
  234.1 4.4 copy-start.1
  240.4 1.8 copy-start.3
  247.9 1.0 copy-start.5
  248.5 5.4 copy-start
  254.6 4.4 copy-start.1
  260.8 1.8 copy-start.3
  268.4 1.0 copy-start.5
  269.0 5.4 copy-start
  275.1 4.4 copy-start.1
  281.3 1.8 copy-start.3
  288.9 1.0 copy-start.5
  289.5 5.4 copy-start
  295.6 4.4 copy-start.1
  301.8 1.8 copy-start.3
  309.3 1.0 copy-start.5
  310.0 5.4 copy-start
  316.1 4.4 copy-start.1
  322.3 1.8 copy-start.3
  329.8 1.0 copy-start.5
  330.5 5.4 copy-start
  336.6 4.4 copy-start.1
  342.8 1.8 copy-start.3
  350.3 1.0 copy-start.5
  351.0 5.4 copy-start
  357.0 4.4 copy-start.1
  363.3 1.8 copy-start.3
  371.4 5.4 copy-start
  377.5 4.4 copy-start.1
  383.8 1.8 copy-start.3
  391.9 5.4 copy-start
  398.0 4.4 copy-start.1
  404.3 1.8 copy-start.3
  412.4 5.4 copy-start
  418.5 4.4 copy-start.1
  424.7 1.8 copy-start.3
  432.9 5.4 copy-start
  439.0 4.4 copy-start.1
  445.2 1.8 copy-start.3
  452.7 1.0 copy-start.5
  453.4 5.4 copy-start
  459.5 4.4 copy-start.1
  465.7 1.8 copy-start.3
  473.9 5.4 copy-start
  480.0 4.4 copy-start.1
  486.2 1.8 copy-start.3
  489.4 82.5 %collective-permute-start.2 = (f32[3,1,384]{2,1,0:T(1,128)S(1)}, f32[3,1,384]{2,1,0:T(1,128)S(1)}, u32[]{:S(2)}, u32[]{:S(2)}) collective-permute-start(f32[3,1,384]{2,1,0:T(1,128)S(1)} %slice.41), channel_id=1, source_target_pairs={{0,1},{1,2},{2,3},{3,4},{4,5},{5,6},{6,7},{7,8},{8,9},{9,10},{10,1... | collective-permute-start | bytes 13832 | tf_op jit(solution)/shard_map/ppermute | solution.py:14
  (37 other events, 24.3 us)
Sparse Core Ops, SparseCore 0:
  9.8 151.1 all-gather.1
where the time goes:
time: 586 us; the launch traced here: 581 us
  matrix products  151 us (26%)
  blocking collectives  118 us (20%)
  waiting for transfers between devices  100 us (17%)
  local copies, waits for them, and re-layouts  94.3 us (16%)
  other arithmetic  77.4 us (13%)
  between operations  15.9 us (3%)
  loops' own time  12.7 us (2%)
  starting transfers between devices  11.9 us (2%)
    all_gather x1, waiting for transfers between devices, on_device(): piece_emb = lax.all_gather(embeddings, 'track', axis=2, tiled=True)  97 us
    dot_general x16, matrix products, tile_terms(): jnp.einsum('fei,fej->fij', emb_a, emb_b, precision=highest) * inv_root  80.6 us
    psum x1, blocking collectives, on_device(): total = lax.psum(energy_sum, ('track', 'tm'))  77 us
    dot_general x16, matrix products, tile_terms(): jnp.einsum('fij,fej->fei', grad_logit, emb_b, precision=highest)  70.5 us
    all_gather x1, blocking collectives, on_device(): piece_packed = lax.all_gather(packed, 'track', axis=2, tiled=True)  41.1 us
    reduce_sum x16, other arithmetic, tile_terms(): grad_pos_a = jnp.sum(scaled, axis=3)  28.8 us
    while x224, local copies, waits for them, and re-layouts  24.9 us
    reduce_sum x16, other arithmetic, tile_terms(): distance = jnp.sqrt(jnp.sum(offset * offset, axis=0) + 1.0)  24.9 us
  transfers between devices with their start and end apart: 4, of which 2 were waited for; matrix products, arithmetic and copies ran while one was open for 1% of the time, Pallas kernels for 0%

commit v1 on v0

--- a/solution.py
+++ b/solution.py
@@ -84,7 +84,7 @@
     incoming = shifted(grad_pos[:, -1:], "tm", 1)
     grad_positions = grad_pos[:, :-1]
     grad_positions = jnp.concatenate([grad_positions[:, :1] + incoming, grad_positions[:, 1:]], 1)
-    total = lax.psum(energy_sum, ("track", "tm"))
+    total = lax.psum(lax.psum(energy_sum, "tm"), "track")
     mean_loss = total / (tracks * (tracks - 1) / 2.0 * (frames - 1))
     return (grad_positions, grad_emb, mean_loss)
 

time: 586 us -> 576 us (0.983)
  the two profiles are of different devices: /device:TPU:1 before, /device:TPU:4 now
where the time goes in v1:
time: 576 us; the launch traced here: 571 us
  matrix products  150 us (26%)
  blocking collectives  121 us (21%)
  local copies, waits for them, and re-layouts  94.2 us (16%)
  waiting for transfers between devices  93.5 us (16%)
  other arithmetic  77.4 us (13%)
  between operations  15.9 us (3%)
  loops' own time  10.9 us (2%)
  starting transfers between devices  8.81 us (2%)
    all_gather x1, waiting for transfers between devices, on_device(): piece_emb = lax.all_gather(embeddings, 'track', axis=2, tiled=True)  92.2 us
    dot_general x16, matrix products, tile_terms(): jnp.einsum('fei,fej->fij', emb_a, emb_b, precision=highest) * inv_root  79.7 us
    psum x2, blocking collectives, on_device(): total = lax.psum(lax.psum(energy_sum, 'tm'), 'track')  72.6 us
    dot_general x16, matrix products, tile_terms(): jnp.einsum('fij,fej->fei', grad_logit, emb_b, precision=highest)  70.5 us
    all_gather x1, blocking collectives, on_device(): piece_packed = lax.all_gather(packed, 'track', axis=2, tiled=True)  48.1 us
    reduce_sum x16, other arithmetic, tile_terms(): grad_pos_a = jnp.sum(scaled, axis=3)  28.8 us
    reduce_sum x16, other arithmetic, tile_terms(): distance = jnp.sqrt(jnp.sum(offset * offset, axis=0) + 1.0)  24.9 us
    while x224, local copies, waits for them, and re-layouts  24.9 us
  transfers between devices with their start and end apart: 4, of which 2 were waited for; matrix products, arithmetic and copies ran while one was open for 1% of the time, Pallas kernels for 0%

profile of v1, /device:TPU:4, one launch (start us, length us, event | category | flops | bytes accessed | tf_op | source)
XLA Modules:
  0.0 571.5 jit_solution(14296015788549141379)
XLA Ops:
  7.2 1.9 copy.30
  9.8 4.3 collective-permute-start
  14.9 2.6 collective-permute-start.1
  19.5 48.1 %all_gather.7 = f32[4,3,6144]{2,1,0:T(4,128)S(1)} all-gather(f32[4,3,384]{2,1,0:T(4,128)S(1)} %pad_maximum_fusion), channel_id=1, replica_groups=mesh['track'=16,'tm'=16] {'track'}, dimensions={2}, use_global_device_ids=true | all-gather | bytes 313344 | tf_op jit(solution)/shard_map/all_gather | solution.py:66
  69.1 92.2 %all-gather.2.cloned.1.call-done = f32[2,128,6144]{1,2,0:T(8,128)} async-done(((f32[2,128,384]{1,2,0:T(8,128)}), f32[2,128,6144]{1,2,0:T(8,128)}) %all-gather.2.cloned.1.call-update) | async-done | bytes 6291472 | tf_op jit(solution)/shard_map/all_gather | solution.py:67
  161.3 324.9 %while.15 = (s32[]{:T(128)}, f32[3,3,384]{2,1,0:T(4,128)}, f32[2,128,384]{2,1,0:T(8,128)}, f32[]{:T(128)}, f32[16,2,128,384]{2,3,0,1:T(8,128)}, /*index=5*/f32[2...) while((s32[]{:T(128)}, f32[3,3,384]{2,1,0:T(4,128)}, ...), condition=%wide.region_4.5_spmd.clone, body=%wide.region_0.4_spmd.clone.sunk | while | flops 922389888 | bytes 49315164 | solution.py:81
  167.3 5.0 multiply_reduce_fusion.2
  172.9 4.3 convolution_add_fusion.2
  179.1 1.8 fusion.35
  183.8 1.6 fusion.34
  187.6 5.0 multiply_reduce_fusion.2
  193.1 4.4 convolution_add_fusion.2
  199.4 1.8 fusion.35
  204.1 1.6 fusion.34
  207.9 5.0 multiply_reduce_fusion.2
  213.4 4.4 convolution_add_fusion.2
  219.7 1.8 fusion.35
  224.4 1.6 fusion.34
  228.2 5.0 multiply_reduce_fusion.2
  233.7 4.4 convolution_add_fusion.2
  240.0 1.8 fusion.35
  244.7 1.6 fusion.34
  248.5 5.0 multiply_reduce_fusion.2
  254.1 4.4 convolution_add_fusion.2
  260.3 1.8 fusion.35
  265.0 1.6 fusion.34
  268.8 5.0 multiply_reduce_fusion.2
  274.4 4.4 convolution_add_fusion.2
  280.6 1.8 fusion.35
  285.4 1.6 fusion.34
  289.1 5.0 multiply_reduce_fusion.2
  294.7 4.4 convolution_add_fusion.2
  300.9 1.8 fusion.35
  305.7 1.6 fusion.34
  309.4 5.0 multiply_reduce_fusion.2
  315.0 4.4 convolution_add_fusion.2
  321.2 1.8 fusion.35
  329.7 5.0 multiply_reduce_fusion.2
  335.3 4.4 convolution_add_fusion.2
  341.5 1.8 fusion.35
  350.0 5.0 multiply_reduce_fusion.2
  355.6 4.4 convolution_add_fusion.2
  361.9 1.8 fusion.35
  370.4 5.0 multiply_reduce_fusion.2
  375.9 4.4 convolution_add_fusion.2
  382.2 1.8 fusion.35
  390.7 5.0 multiply_reduce_fusion.2
  396.2 4.4 convolution_add_fusion.2
  402.5 1.8 fusion.35
  411.0 5.0 multiply_reduce_fusion.2
  416.5 4.4 convolution_add_fusion.2
  422.8 1.8 fusion.35
  431.3 5.0 multiply_reduce_fusion.2
  436.9 4.4 convolution_add_fusion.2
  443.1 1.8 fusion.35
  451.6 5.0 multiply_reduce_fusion.2
  457.2 4.4 convolution_add_fusion.2
  463.4 1.8 fusion.35
  471.9 5.0 multiply_reduce_fusion.2
  477.5 4.4 convolution_add_fusion.2
  483.7 1.8 fusion.35
  486.9 1.9 collective-permute-start.2
  488.8 39.0 %psum.14 = f32[]{:T(128)} all-reduce(f32[]{:T(128)S(6)} %mul_shard_map.3), channel_id=1, replica_groups=mesh['track'=16,'tm'=16] {'tm'}, use_global_device_ids=true, to_apply=%region_5.6 | all-reduce | flops 1 | bytes 8 | tf_op jit(solution)/shard_map/psum | solution.py:87
  527.8 33.6 %psum.15 = f32[]{:T(128)} all-reduce(f32[]{:T(128)} %psum.14), channel_id=1, replica_groups=mesh['track'=16,'tm'=16] {'track'}, use_global_device_ids=true, to_apply=%region_6.7 | all-reduce | flops 1 | bytes 8 | tf_op jit(solution)/shard_map/psum | solution.py:87
  (364 shorter events, 131.3 us)
Async XLA Ops:
  7.2 61.3 %copy-start.6 = (f32[3,2,384]{2,1,0:T(2,128)S(1)}, f32[3,2,384]{2,1,0:T(2,128)}, u32[]{:S(2)}) copy-start(f32[3,2,384]{2,1,0:T(2,128)} %param.5) | copy-start | bytes 27652
  7.2 154.1 %all-gather.2.cloned.1.call-start = ((), (), s32[]{:S(2)}) async-start(), calls=%async_computation | async-start | bytes 6684672 | tf_op jit(solution)/shard_map/all_gather | solution.py:67
  9.8 7.6 %collective-permute-start = (f32[1,384]{1,0:T(1,128)S(1)}, f32[1,384]{1,0:T(1,128)S(1)}, u32[]{:S(2)}, u32[]{:S(2)}) collective-permute-start(f32[1,384]{1,0:T(1,128)S(1)} %slice.53), channel_id=1, source_target_pairs={{1,0},{2,1},{3,2},{4,3},{5,4},{6,5},{7,6},{8,7},{9,8},{10,9},{11,1... | collective-permute-start | bytes 4616 | tf_op jit(solution)/shard_map/ppermute | solution.py:14
  14.9 3.9 collective-permute-start.1
  166.3 1.0 copy-start.5
  167.0 5.3 copy-start
  172.9 4.3 copy-start.1
  179.0 1.8 copy-start.3
  186.6 1.0 copy-start.5
  187.2 5.3 copy-start
  193.1 4.4 copy-start.1
  199.4 1.8 copy-start.3
  206.9 1.0 copy-start.5
  207.5 5.3 copy-start
  213.4 4.4 copy-start.1
  219.7 1.8 copy-start.3
  227.2 1.0 copy-start.5
  227.8 5.3 copy-start
  233.7 4.4 copy-start.1
  240.0 1.8 copy-start.3
  248.1 5.3 copy-start
  254.0 4.4 copy-start.1
  260.3 1.8 copy-start.3
  268.4 5.3 copy-start
  274.4 4.4 copy-start.1
  280.6 1.8 copy-start.3
  288.8 5.3 copy-start
  294.7 4.4 copy-start.1
  300.9 1.8 copy-start.3
  308.4 1.0 copy-start.5
  309.1 5.3 copy-start
  315.0 4.4 copy-start.1
  321.2 1.8 copy-start.3
  328.7 1.0 copy-start.5
  329.4 5.3 copy-start
  335.3 4.4 copy-start.1
  341.5 1.8 copy-start.3
  349.0 1.0 copy-start.5
  349.7 5.3 copy-start
  355.6 4.4 copy-start.1
  361.8 1.8 copy-start.3
  369.4 1.0 copy-start.5
  370.0 5.3 copy-start
  375.9 4.4 copy-start.1
  382.2 1.8 copy-start.3
  389.7 1.0 copy-start.5
  390.3 5.3 copy-start
  396.2 4.4 copy-start.1
  402.5 1.8 copy-start.3
  410.0 1.0 copy-start.5
  410.6 5.3 copy-start
  416.5 4.4 copy-start.1
  422.8 1.8 copy-start.3
  430.3 1.0 copy-start.5
  430.9 5.3 copy-start
  436.8 4.4 copy-start.1
  443.1 1.8 copy-start.3
  451.3 5.3 copy-start
  457.2 4.4 copy-start.1
  463.4 1.8 copy-start.3
  471.6 5.3 copy-start
  477.5 4.4 copy-start.1
  483.7 1.8 copy-start.3
  486.9 75.2 %collective-permute-start.2 = (f32[3,1,384]{2,1,0:T(1,128)S(1)}, f32[3,1,384]{2,1,0:T(1,128)S(1)}, u32[]{:S(2)}, u32[]{:S(2)}) collective-permute-start(f32[3,1,384]{2,1,0:T(1,128)S(1)} %slice.41), channel_id=1, source_target_pairs={{0,1},{1,2},{2,3},{3,4},{4,5},{5,6},{6,7},{7,8},{8,9},{9,10},{10,1... | collective-permute-start | bytes 13832 | tf_op jit(solution)/shard_map/ppermute | solution.py:14
  (37 other events, 24.2 us)
Sparse Core Ops, SparseCore 0:
  9.8 151.4 all-gather.1
